TPU v7x, 256 devices: a whole 4x4x8 slice. The times are simulated.
256 devices in a mesh: seq: 32 (over z, y), head: 8 (over x, core).
Axes of the slice: x: 4, y: 4, z: 8, core: 2. Of those that a mesh axis runs over, the one named last changes fastest.
Arguments:
- query_in: bfloat16 [32768, 32, 128], P(('seq', 'head')), may hold values from -6 to 6
- key_in: bfloat16 [32768, 32, 128], P(('seq', 'head')), may hold values from -6 to 6
- value_in: bfloat16 [32768, 32, 128], P(('seq', 'head')), may hold values from -6 to 6
- grad_out: bfloat16 [32768, 32, 128], P(('seq', 'head')), may hold values from -6 to 6
- log_decay: bfloat16 [32768, 32], P(('seq', 'head')), may hold values from -1 to 0, as said below
Outputs:
- attended: bfloat16 [32768, 32, 128], P(('seq', 'head'))
- grad_query: bfloat16 [32768, 32, 128], P(('seq', 'head'))
- grad_key: bfloat16 [32768, 32, 128], P(('seq', 'head'))
- grad_value: bfloat16 [32768, 32, 128], P(('seq', 'head'))
Inputs may be any that keep to these rules, and one draw needn't show every extreme that they name: Every entry of log_decay is negative.
All inputs are finite; a program needn't handle non-finite values.
Results may differ from a plain program's by a relative error of at most 0.007.
Values may be sent and summed in bfloat16 or wider, within the bound.
A program may use at most 128 MiB of HBM per device.

v0:
```python
import jax
import jax.numpy as jnp
from jax import lax
from jax.sharding import PartitionSpec as P

precise = lax.Precision.HIGHEST


def shards(query_in, key_in, value_in, grad_out, log_decay):
    f32 = jnp.float32
    bf16 = jnp.bfloat16
    queries, keys_all, values, grads, token_decays = (
        lax.all_to_all(query_in, "head", split_axis=1, concat_axis=0, tiled=True),
        lax.all_to_all(key_in, "head", split_axis=1, concat_axis=0, tiled=True),
        lax.all_to_all(value_in, "head", split_axis=1, concat_axis=0, tiled=True),
        lax.all_to_all(grad_out, "head", split_axis=1, concat_axis=0, tiled=True),
        lax.all_to_all(log_decay, "head", split_axis=1, concat_axis=0, tiled=True),
    )
    segment_length = queries.shape[0]
    width = queries.shape[2]
    scaling = 1.0 / width
    within = jnp.cumsum(token_decays.astype(f32), axis=0)
    seg_total = within[-1]
    to_start = jnp.exp(within)[:, :, None]
    to_end = jnp.exp(seg_total[None, :] - within)[:, :, None]
    keys_end = (keys_all.astype(f32) * to_end).astype(bf16)
    values_end = (values.astype(f32) * to_end).astype(bf16)
    queries_start = (queries.astype(f32) * to_start).astype(bf16)
    grads_start = (grads.astype(f32) * to_start).astype(bf16)
    local_kv = jnp.einsum("thd,the->hde", keys_end, values, preferred_element_type=f32).astype(bf16)
    local_qg = jnp.einsum("thd,the->hde", queries_start, grads, preferred_element_type=f32).astype(
        bf16
    )
    seg_count = lax.axis_size("seq")
    seq_place = lax.axis_index("seq")
    totals = lax.all_gather(seg_total[None, :], "seq", axis=0, tiled=True)
    cum_inc = jnp.cumsum(totals, axis=0)
    cum_exc = cum_inc - totals
    mine_inc = lax.dynamic_index_in_dim(cum_inc, seq_place, 0, keepdims=False)
    mine_exc = lax.dynamic_index_in_dim(cum_exc, seq_place, 0, keepdims=False)
    ranks = jnp.arange(seg_count)[:, None]
    earlier = ranks < seq_place
    later_on = ranks > seq_place
    w_in = jnp.where(earlier, jnp.exp(jnp.where(earlier, mine_exc[None, :] - cum_inc, 0.0)), 0.0)
    w_out = jnp.where(later_on, jnp.exp(jnp.where(later_on, cum_exc - mine_inc[None, :], 0.0)), 0.0)
    new_in = jnp.einsum(
        "ih,ihde->hde",
        w_in,
        lax.all_gather(local_kv[None], "seq", axis=0, tiled=True).astype(f32),
        precision=precise,
    )
    new_out = jnp.einsum(
        "ih,ihde->hde",
        w_out,
        lax.all_gather(local_qg[None], "seq", axis=0, tiled=True).astype(f32),
        precision=precise,
    )
    state_in = new_in
    state_out = new_out
    state_in = state_in.astype(bf16)
    state_out = state_out.astype(bf16)
    head_specific = within.T
    causal = jnp.arange(segment_length)[:, None] >= jnp.arange(segment_length)[None, :]
    decay_mat = jnp.where(
        causal,
        jnp.exp(jnp.where(causal, head_specific[:, :, None] - head_specific[:, None, :], 0.0)),
        0.0,
    )
    scores = jnp.einsum("thd,shd->hts", queries, keys_all, preferred_element_type=f32)
    attn_w = (scaling * scores * decay_mat).astype(bf16)
    intra = jnp.einsum("hts,shd->thd", attn_w, values, preferred_element_type=f32)
    attended = (
        intra
        + scaling * jnp.einsum("thd,hde->the", queries_start, state_in, preferred_element_type=f32)
    ).astype(bf16)
    back_raw = jnp.einsum("the,she->hts", grads, values, preferred_element_type=f32)
    back_w = (scaling * back_raw * decay_mat).astype(bf16)
    grad_query = (
        jnp.einsum("hts,shd->thd", back_w, keys_all, preferred_element_type=f32)
        + scaling * jnp.einsum("the,hde->thd", grads_start, state_in, preferred_element_type=f32)
    ).astype(bf16)
    grad_key = (
        jnp.einsum("hts,thd->shd", back_w, queries, preferred_element_type=f32)
        + scaling * jnp.einsum("she,hde->shd", values_end, state_out, preferred_element_type=f32)
    ).astype(bf16)
    grad_value = (
        jnp.einsum("hts,the->she", attn_w, grads, preferred_element_type=f32)
        + scaling * jnp.einsum("shd,hde->she", keys_end, state_out, preferred_element_type=f32)
    ).astype(bf16)
    results = (
        lax.all_to_all(attended, "head", split_axis=0, concat_axis=1, tiled=True),
        lax.all_to_all(grad_query, "head", split_axis=0, concat_axis=1, tiled=True),
        lax.all_to_all(grad_key, "head", split_axis=0, concat_axis=1, tiled=True),
        lax.all_to_all(grad_value, "head", split_axis=0, concat_axis=1, tiled=True),
    )
    return (results[0], results[1], results[2], results[3])


def solution(mesh):
    return jax.shard_map(
        shards,
        mesh=mesh,
        in_specs=(
            P(("seq", "head"), None, None),
            P(("seq", "head"), None, None),
            P(("seq", "head"), None, None),
            P(("seq", "head"), None, None),
            P(("seq", "head"), None),
        ),
        out_specs=(
            P(("seq", "head"), None, None),
            P(("seq", "head"), None, None),
            P(("seq", "head"), None, None),
            P(("seq", "head"), None, None),
        ),
        check_vma=False,
    )
```

profile of v0, /device:TPU:1, one launch (start us, length us, event | category | flops | bytes accessed | tf_op | source)
XLA Modules:
  0.0 301.6 jit_solution(2192634646455913351)
XLA Ops:
  7.2 6.6 %all-to-all-start.2 = ((bf16[128,8,4]{0,2,1:T(4,128)(2,1)}), bf16[128,8,4]{0,2,1:T(4,128)(2,1)S(1)}, u32[]{:S(2)}, u32[]{:S(2)}) async-start(bf16[128,8,4]{0,2,1:T(4,128)(2,1)} %bitcast.154), calls=%async_computation.2 | async-start | bytes 16384 | tf_op jit(solution)/shard_map/all_to_all | solution.py:17
  13.8 2.6 copy.120
  16.4 2.0 all-to-all-done.2
  18.4 4.2 %all-to-all-start.1 = ((bf16[128,32,128]{2,0,1:T(8,128)(2,1)}), bf16[128,32,128]{2,0,1:T(8,128)(2,1)S(1)}, u32[]{:S(2)}, u32[]{:S(2)}) async-start(bf16[128,32,128]{2,0,1:T(8,128)(2,1)} %copy.120), calls=%async_computation.1 | async-start | bytes 2097152 | tf_op jit(solution)/shard_map/all_to_all | solution.py:14
  22.6 1.4 copy.122
  24.0 13.7 %all-to-all-done.1 = bf16[128,32,128]{2,0,1:T(8,128)(2,1)S(1)} async-done(((bf16[128,32,128]{2,0,1:T(8,128)(2,1)}), bf16[128,32,128]{2,0,1:T(8,128)(2,1)S(1)}, u32[]{:S(2)}, u32[]{:S(2)}) %all-to-all-start.1) | async-done | bytes 1048608 | tf_op jit(solution)/shard_map/all_to_all | solution.py:14
  37.7 4.3 %all-to-all-start.3 = ((bf16[128,32,128]{2,0,1:T(8,128)(2,1)}), bf16[128,32,128]{2,0,1:T(8,128)(2,1)S(1)}, u32[]{:S(2)}, u32[]{:S(2)}) async-start(bf16[128,32,128]{2,0,1:T(8,128)(2,1)} %copy.122), calls=%async_computation.3 | async-start | bytes 2097152 | tf_op jit(solution)/shard_map/all_to_all | solution.py:15
  42.1 1.1 reduce-window.6
  44.0 13.1 %all-to-all-done.3 = bf16[128,32,128]{2,0,1:T(8,128)(2,1)S(1)} async-done(((bf16[128,32,128]{2,0,1:T(8,128)(2,1)}), bf16[128,32,128]{2,0,1:T(8,128)(2,1)S(1)}, u32[]{:S(2)}, u32[]{:S(2)}) %all-to-all-start.3) | async-done | bytes 1048608 | tf_op jit(solution)/shard_map/all_to_all | solution.py:15
  57.3 1.0 copy-done.4
  58.2 2.0 convolution_convert_fusion.1
  60.3 2.6 copy.118
  62.9 4.3 %all-to-all-start = ((bf16[128,32,128]{2,0,1:T(8,128)(2,1)}), bf16[128,32,128]{2,0,1:T(8,128)(2,1)S(1)}, u32[]{:S(2)}, u32[]{:S(2)}) async-start(bf16[128,32,128]{2,0,1:T(8,128)(2,1)} %copy.118), calls=%async_computation | async-start | bytes 2097152 | tf_op jit(solution)/shard_map/all_to_all | solution.py:13
  67.2 1.4 copy.132
  68.6 13.7 %all-to-all-done = bf16[128,32,128]{2,0,1:T(8,128)(2,1)S(1)} async-done(((bf16[128,32,128]{2,0,1:T(8,128)(2,1)}), bf16[128,32,128]{2,0,1:T(8,128)(2,1)S(1)}, u32[]{:S(2)}, u32[]{:S(2)}) %all-to-all-start) | async-done | bytes 1048608 | tf_op jit(solution)/shard_map/all_to_all | solution.py:13
  82.3 4.3 %all-to-all-start.5 = ((bf16[128,32,128]{2,0,1:T(8,128)(2,1)}), bf16[128,32,128]{2,0,1:T(8,128)(2,1)S(1)}, u32[]{:S(2)}, u32[]{:S(2)}) async-start(bf16[128,32,128]{2,0,1:T(8,128)(2,1)} %copy.132), calls=%async_computation.5 | async-start | bytes 2097152 | tf_op jit(solution)/shard_map/all_to_all | solution.py:16
  86.8 15.0 %all-to-all-done.5 = bf16[128,32,128]{2,0,1:T(8,128)(2,1)S(1)} async-done(((bf16[128,32,128]{2,0,1:T(8,128)(2,1)}), bf16[128,32,128]{2,0,1:T(8,128)(2,1)S(1)}, u32[]{:S(2)}, u32[]{:S(2)}) %all-to-all-start.5) | async-done | bytes 1048608 | tf_op jit(solution)/shard_map/all_to_all | solution.py:16
  101.9 2.0 convolution_convert_fusion
  104.2 37.7 %all-gather.2 = f32[32,1,4]{2,1,0:T(1,128)S(1)} all-gather(f32[1,1,4]{2,1,0:T(1,128)S(1)} %bitcast.155), channel_id=1, replica_groups=mesh['seq'=32,'head'=8] {'seq'}, dimensions={0}, use_global_device_ids=true | all-gather | bytes 528 | tf_op jit(solution)/shard_map/all_gather | solution.py:36
  142.4 7.4 %multiply_convert_fusion = bf16[4,1024,1024]{2,1,0:T(8,128)(2,1)S(1)} fusion(bf16[1024,4,128]{2,0,1:T(8,128)(2,1)S(1)} %bitcast.118, bf16[1024,4,128]{2,0,1:T(8,128)(2,1)} %bitcast.139, f32[4,1024]{1,0:T(4,128)S(1)} %bitcast.150, pred[1024,1024]{1,0:T(8,128)(4,1)S(1)} %iota_compare_fusion), kind=kOutput, calls=%fused_computation | convolution fusion | flops 1098907648 | bytes 11550720 | tf_op jit(solution)/shard_map/the,she->hts/dot_general | solution.py:76
  149.8 4.0 %fusion.14 = f32[4,1024,128]{2,1,0:T(8,128)} fusion(bf16[4,1024,1024]{2,1,0:T(8,128)(2,1)S(1)} %multiply_convert_fusion, bf16[1024,4,128]{2,0,1:T(8,128)(2,1)S(1)} %bitcast.135), kind=kOutput, calls=%fused_computation.43 | convolution fusion | flops 1073741824 | bytes 11534336 | tf_op jit(solution)/shard_map/hts,shd->thd/dot_general | solution.py:79
  153.8 7.8 %multiply_convert_fusion.1 = bf16[4,1024,1024]{2,1,0:T(8,128)(2,1)} fusion(bf16[1024,4,128]{2,0,1:T(8,128)(2,1)S(1)} %bitcast.122, bf16[1024,4,128]{2,0,1:T(8,128)(2,1)S(1)} %bitcast.136, f32[4,1024]{1,0:T(4,128)S(1)} %bitcast.151, pred[1024,1024]{1,0:T(8,128)(4,1)S(1)} %iota_compare_fusion), kind=kOutput, calls=%fused_computation.1 | convolution fusion | flops 1098907648 | bytes 11550720 | tf_op jit(solution)/shard_map/thd,shd->hts/dot_general | solution.py:69
  161.6 5.8 %fusion = f32[4,1,128,128]{3,1,2,0:T(1,128)S(1)} fusion(f32[32,4,1,1]{0,2,3,1:T(1,128)S(1)} %copy.148, bf16[32,4,128,128]{3,2,1,0:T(8,128)(2,1)} %bitcast.125), kind=kOutput, calls=%fused_computation.4 | convolution fusion | flops 25165824 | bytes 4456960 | tf_op jit(solution)/shard_map/ih,ihde->hde/dot_general | solution.py:46
  167.4 1.0 fusion.4
  168.4 1.8 copy.135
  170.2 8.2 %all-to-all-start.6 = ((bf16[1024,4,128]{2,1,0:T(4,128)(2,1)}), bf16[1024,4,128]{2,1,0:T(4,128)(2,1)S(1)}, u32[]{:S(2)}, u32[]{:S(2)}) async-start(bf16[1024,4,128]{2,1,0:T(4,128)(2,1)} %copy.135), calls=%async_computation.6 | async-start | bytes 2097152 | tf_op jit(solution)/shard_map/all_to_all | solution.py:92
  178.4 7.7 %fusion.15 = f32[4,1024,128]{2,1,0:T(8,128)} fusion(bf16[4,1024,1024]{2,1,0:T(8,128)(2,1)} %copy-done, bf16[1024,4,128]{2,0,1:T(8,128)(2,1)S(1)} %bitcast.123), kind=kOutput, calls=%fused_computation.44 | convolution fusion | flops 1073741824 | bytes 11534336 | tf_op jit(solution)/shard_map/hts,thd->shd/dot_general | solution.py:83
  186.1 36.4 %all-gather.8.cloned.1.call-done = bf16[128,128,128]{2,1,0:T(8,128)(2,1)} async-done(((bf16[4,128,128]{2,1,0:T(8,128)(2,1)}), bf16[128,128,128]{2,1,0:T(8,128)(2,1)}) %all-gather.8.cloned.1.call-update) | async-done | bytes 4194320 | tf_op jit(solution)/shard_map/all_gather | solution.py:55
  222.5 3.7 %multiply_reduce_fusion = bf16[4,128,128]{2,1,0:T(8,128)(2,1)} fusion(bf16[4,32,128,128]{3,2,0,1:T(8,128)(2,1)} %bitcast.126, f32[4,32]{0,1:T(8,128)S(1)} %get-tuple-element.4), kind=kLoop, calls=%fused_computation.3 | loop fusion | flops 6225920 | bytes 4325888
  226.3 1.0 copy.162
  227.3 2.7 fusion.3
  230.0 1.8 copy.141
  231.8 7.6 %all-to-all-start.7 = ((bf16[1024,4,128]{2,1,0:T(4,128)(2,1)}), bf16[1024,4,128]{2,1,0:T(4,128)(2,1)}, u32[]{:S(2)}, u32[]{:S(2)}) async-start(bf16[1024,4,128]{2,1,0:T(4,128)(2,1)} %copy.141), calls=%async_computation.7 | async-start | bytes 2097152 | tf_op jit(solution)/shard_map/all_to_all | solution.py:93
  239.3 5.9 %fusion.13 = f32[4,1024,128]{2,1,0:T(8,128)S(1)} fusion(bf16[4,1024,1024]{2,1,0:T(8,128)(2,1)} %multiply_convert_fusion.1, bf16[1024,4,128]{2,0,1:T(8,128)(2,1)} %bitcast.141), kind=kOutput, calls=%fused_computation.42 | convolution fusion | flops 1073741824 | bytes 11534336 | tf_op jit(solution)/shard_map/hts,shd->thd/dot_general | solution.py:71
  245.3 1.0 fusion.5
  246.3 1.8 copy.130
  248.1 6.5 %all-to-all-done.7 = bf16[1024,4,128]{2,1,0:T(4,128)(2,1)} async-done(((bf16[1024,4,128]{2,1,0:T(4,128)(2,1)}), bf16[1024,4,128]{2,1,0:T(4,128)(2,1)}, u32[]{:S(2)}, u32[]{:S(2)}) %all-to-all-start.7) | async-done | bytes 1048608 | tf_op jit(solution)/shard_map/all_to_all | solution.py:93
  254.5 4.3 %all-to-all-start.4 = ((bf16[1024,4,128]{2,1,0:T(4,128)(2,1)}), bf16[1024,4,128]{2,1,0:T(4,128)(2,1)S(1)}, u32[]{:S(2)}, u32[]{:S(2)}) async-start(bf16[1024,4,128]{2,1,0:T(4,128)(2,1)} %copy.130), calls=%async_computation.4 | async-start | bytes 2097152 | tf_op jit(solution)/shard_map/all_to_all | solution.py:91
  258.9 6.4 %fusion.16 = f32[4,1024,128]{2,1,0:T(8,128)S(1)} fusion(bf16[4,1024,1024]{2,1,0:T(8,128)(2,1)} %multiply_convert_fusion.1, bf16[1024,4,128]{2,0,1:T(8,128)(2,1)S(1)} %bitcast.120), kind=kOutput, calls=%fused_computation.45 | convolution fusion | flops 1073741824 | bytes 11534336 | tf_op jit(solution)/shard_map/hts,the->she/dot_general | solution.py:87
  265.3 1.0 fusion.2
  266.3 1.8 copy.145
  268.1 5.9 %all-to-all-done.4 = bf16[1024,4,128]{2,1,0:T(4,128)(2,1)S(1)} async-done(((bf16[1024,4,128]{2,1,0:T(4,128)(2,1)}), bf16[1024,4,128]{2,1,0:T(4,128)(2,1)S(1)}, u32[]{:S(2)}, u32[]{:S(2)}) %all-to-all-start.4) | async-done | bytes 1048608 | tf_op jit(solution)/shard_map/all_to_all | solution.py:91
  274.0 4.3 %all-to-all-start.8 = ((bf16[1024,4,128]{2,1,0:T(4,128)(2,1)}), bf16[1024,4,128]{2,1,0:T(4,128)(2,1)S(1)}, u32[]{:S(2)}, u32[]{:S(2)}) async-start(bf16[1024,4,128]{2,1,0:T(4,128)(2,1)} %copy.145), calls=%async_computation.8 | async-start | bytes 2097152 | tf_op jit(solution)/shard_map/all_to_all | solution.py:94
  278.3 1.3 copy.136
  279.6 2.6 copy.142
  282.2 1.3 copy.131
  283.5 9.9 %all-to-all-done.8 = bf16[1024,4,128]{2,1,0:T(4,128)(2,1)S(1)} async-done(((bf16[1024,4,128]{2,1,0:T(4,128)(2,1)}), bf16[1024,4,128]{2,1,0:T(4,128)(2,1)S(1)}, u32[]{:S(2)}, u32[]{:S(2)}) %all-to-all-start.8) | async-done | bytes 1048608 | tf_op jit(solution)/shard_map/all_to_all | solution.py:94
  293.4 1.3 copy.146
  (47 shorter events, 2.0 us)
Async XLA Ops:
  7.2 15.4 %copy-start.6 = (bf16[128,32,128]{2,1,0:T(8,128)(2,1)S(1)}, bf16[128,32,128]{2,1,0:T(8,128)(2,1)}, u32[]{:S(2)}) copy-start(bf16[128,32,128]{2,1,0:T(8,128)(2,1)} %param.7) | copy-start | bytes 3145732
  7.2 11.3 %all-to-all-start.2 = ((bf16[128,8,4]{0,2,1:T(4,128)(2,1)}), bf16[128,8,4]{0,2,1:T(4,128)(2,1)S(1)}, u32[]{:S(2)}, u32[]{:S(2)}) async-start(bf16[128,8,4]{0,2,1:T(4,128)(2,1)} %bitcast.154), calls=%async_computation.2 | async-start | bytes 16384 | tf_op jit(solution)/shard_map/all_to_all | solution.py:17
  18.4 19.3 %all-to-all-start.1 = ((bf16[128,32,128]{2,0,1:T(8,128)(2,1)}), bf16[128,32,128]{2,0,1:T(8,128)(2,1)S(1)}, u32[]{:S(2)}, u32[]{:S(2)}) async-start(bf16[128,32,128]{2,0,1:T(8,128)(2,1)} %copy.120), calls=%async_computation.1 | async-start | bytes 2097152 | tf_op jit(solution)/shard_map/all_to_all | solution.py:14
  37.7 19.5 %all-to-all-start.3 = ((bf16[128,32,128]{2,0,1:T(8,128)(2,1)}), bf16[128,32,128]{2,0,1:T(8,128)(2,1)S(1)}, u32[]{:S(2)}, u32[]{:S(2)}) async-start(bf16[128,32,128]{2,0,1:T(8,128)(2,1)} %copy.122), calls=%async_computation.3 | async-start | bytes 2097152 | tf_op jit(solution)/shard_map/all_to_all | solution.py:15
  42.0 119.5 %all-gather.6.cloned.1.call-start = ((), (), s32[]{:S(2)}) async-start(), calls=%async_computation.9 | async-start | bytes 4325376 | tf_op jit(solution)/shard_map/all_gather | solution.py:49
  43.9 123.5 %copy-start.8 = (f32[1024,4]{0,1:T(4,128)}, f32[1024,4]{0,1:T(4,128)S(1)}, u32[]{:S(2)}) copy-start(f32[1024,4]{0,1:T(4,128)S(1)} %get-tuple-element.7) | copy-start | bytes 49156
  44.0 18.8 %copy-start.1 = (bf16[128,8,4,128]{3,0,1,2:T(8,128)(2,1)}, bf16[128,8,4,128]{3,0,1,2:T(8,128)(2,1)S(1)}, u32[]{:S(2)}) copy-start(bf16[128,8,4,128]{3,0,1,2:T(8,128)(2,1)S(1)} %copy.121) | copy-start | bytes 3145732
  57.3 1.0 copy-start.4
  57.3 9.9 %copy-start.7 = (bf16[128,32,128]{2,1,0:T(8,128)(2,1)S(1)}, bf16[128,32,128]{2,1,0:T(8,128)(2,1)}, u32[]{:S(2)}) copy-start(bf16[128,32,128]{2,1,0:T(8,128)(2,1)} %param.8) | copy-start | bytes 3145732
  62.9 19.5 %all-to-all-start = ((bf16[128,32,128]{2,0,1:T(8,128)(2,1)}), bf16[128,32,128]{2,0,1:T(8,128)(2,1)S(1)}, u32[]{:S(2)}, u32[]{:S(2)}) async-start(bf16[128,32,128]{2,0,1:T(8,128)(2,1)} %copy.118), calls=%async_computation | async-start | bytes 2097152 | tf_op jit(solution)/shard_map/all_to_all | solution.py:13
  82.3 19.5 %all-to-all-start.5 = ((bf16[128,32,128]{2,0,1:T(8,128)(2,1)}), bf16[128,32,128]{2,0,1:T(8,128)(2,1)S(1)}, u32[]{:S(2)}, u32[]{:S(2)}) async-start(bf16[128,32,128]{2,0,1:T(8,128)(2,1)} %copy.132), calls=%async_computation.5 | async-start | bytes 2097152 | tf_op jit(solution)/shard_map/all_to_all | solution.py:16
  86.6 135.9 %all-gather.8.cloned.1.call-start = ((), (), s32[]{:S(2)}) async-start(), calls=%async_computation.10 | async-start | bytes 4325376 | tf_op jit(solution)/shard_map/all_gather | solution.py:55
  142.4 7.4 %copy-start.2 = (bf16[128,8,4,128]{3,0,1,2:T(8,128)(2,1)S(1)}, bf16[128,8,4,128]{3,0,1,2:T(8,128)(2,1)}, u32[]{:S(2)}) copy-start(bf16[128,8,4,128]{3,0,1,2:T(8,128)(2,1)} %copy-done.1) | copy-start | bytes 3145732
  149.8 4.0 %copy-start = (bf16[4,1024,1024]{2,1,0:T(8,128)(2,1)}, bf16[4,1024,1024]{2,1,0:T(8,128)(2,1)S(1)}, u32[]{:S(2)}) copy-start(bf16[4,1024,1024]{2,1,0:T(8,128)(2,1)S(1)} %multiply_convert_fusion) | copy-start | bytes 25165828
  161.6 5.9 %copy-start.5 = (f32[4,1024,128]{2,1,0:T(8,128)S(1)}, f32[4,1024,128]{2,1,0:T(8,128)}, u32[]{:S(2)}) copy-start(f32[4,1024,128]{2,1,0:T(8,128)} %fusion.14) | copy-start | bytes 6291460
  170.2 61.5 %all-to-all-start.6 = ((bf16[1024,4,128]{2,1,0:T(4,128)(2,1)}), bf16[1024,4,128]{2,1,0:T(4,128)(2,1)S(1)}, u32[]{:S(2)}, u32[]{:S(2)}) async-start(bf16[1024,4,128]{2,1,0:T(4,128)(2,1)} %copy.135), calls=%async_computation.6 | async-start | bytes 2097152 | tf_op jit(solution)/shard_map/all_to_all | solution.py:92
  231.8 22.8 %all-to-all-start.7 = ((bf16[1024,4,128]{2,1,0:T(4,128)(2,1)}), bf16[1024,4,128]{2,1,0:T(4,128)(2,1)}, u32[]{:S(2)}, u32[]{:S(2)}) async-start(bf16[1024,4,128]{2,1,0:T(4,128)(2,1)} %copy.141), calls=%async_computation.7 | async-start | bytes 2097152 | tf_op jit(solution)/shard_map/all_to_all | solution.py:93
  239.3 6.0 %copy-start.9 = (f32[1024,4]{0,1:T(4,128)S(1)}, f32[1024,4]{0,1:T(4,128)}, u32[]{:S(2)}) copy-start(f32[1024,4]{0,1:T(4,128)} %copy-done.8) | copy-start | bytes 49156
  254.5 19.5 %all-to-all-start.4 = ((bf16[1024,4,128]{2,1,0:T(4,128)(2,1)}), bf16[1024,4,128]{2,1,0:T(4,128)(2,1)S(1)}, u32[]{:S(2)}, u32[]{:S(2)}) async-start(bf16[1024,4,128]{2,1,0:T(4,128)(2,1)} %copy.130), calls=%async_computation.4 | async-start | bytes 2097152 | tf_op jit(solution)/shard_map/all_to_all | solution.py:91
  258.9 6.4 %copy-start.3 = (bf16[128,8,4,128]{3,0,1,2:T(8,128)(2,1)S(1)}, bf16[128,8,4,128]{3,0,1,2:T(8,128)(2,1)}, u32[]{:S(2)}) copy-start(bf16[128,8,4,128]{3,0,1,2:T(8,128)(2,1)} %copy-done.1) | copy-start | bytes 3145732
  274.0 19.4 %all-to-all-start.8 = ((bf16[1024,4,128]{2,1,0:T(4,128)(2,1)}), bf16[1024,4,128]{2,1,0:T(4,128)(2,1)S(1)}, u32[]{:S(2)}, u32[]{:S(2)}) async-start(bf16[1024,4,128]{2,1,0:T(4,128)(2,1)} %copy.145), calls=%async_computation.8 | async-start | bytes 2097152 | tf_op jit(solution)/shard_map/all_to_all | solution.py:94
Sparse Core Ops, SparseCore 0:
  60.4 79.9 all-gather.5
  143.5 78.9 all-gather.7
where the time goes:
time: 302 us
  waiting for transfers between devices  116 us (38%)
  matrix products  54.6 us (18%)
  starting transfers between devices  48.2 us (16%)
  blocking collectives  37.7 us (12%)
  local copies, waits for them, and re-layouts  24.7 us (8%)
  between operations  14.3 us (5%)
  other arithmetic  5.77 us (2%)
    all_gather x1, blocking collectives, shards(): totals = lax.all_gather(seg_total[None, :], 'seq', axis=0, tiled=True)  37.7 us
    all_gather x1, waiting for transfers between devices, shards(): lax.all_gather(local_qg[None], 'seq', axis=0, tiled=True).astype(f32)  36.4 us
    all_to_all x1, waiting for transfers between devices, shards(): lax.all_to_all(grad_out, 'head', split_axis=1, concat_axis=0, tiled=True)  15 us
    all_to_all x1, waiting for transfers between devices, shards(): lax.all_to_all(key_in, 'head', split_axis=1, concat_axis=0, tiled=True)  13.7 us
    all_to_all x1, waiting for transfers between devices, shards(): lax.all_to_all(query_in, 'head', split_axis=1, concat_axis=0, tiled=True)  13.7 us
    all_to_all x1, waiting for transfers between devices, shards(): lax.all_to_all(value_in, 'head', split_axis=1, concat_axis=0, tiled=True)  13.1 us
    all_to_all x1, waiting for transfers between devices, shards(): lax.all_to_all(grad_value, 'head', split_axis=0, concat_axis=1, tiled=True)  9.9 us
    unnamed x27, local copies, waits for them, and re-layouts  9.06 us
  transfers between devices with their start and end apart: 11, of which 9 were waited for; matrix products, arithmetic and copies ran while one was open for 27% of the time, Pallas kernels for 0%

commit v1 on v0

--- a/solution.py
+++ b/solution.py
@@ -52,7 +52,9 @@
     new_out = jnp.einsum(
         "ih,ihde->hde",
         w_out,
-        lax.all_gather(local_qg[None], "seq", axis=0, tiled=True).astype(f32),
+        jnp.concatenate(
+            lax.all_to_all(jnp.stack([local_qg[None]] * lax.axis_size("seq")), "seq", 0, 0), axis=0
+        ).astype(f32),
         precision=precise,
     )
     state_in = new_in

time: 302 us -> 376 us (1.25)
  blocking collectives: 37.7 us -> 136 us
  waiting for transfers between devices: 116 us -> 74.4 us
  starting transfers between devices: 48.2 us -> 60.7 us
  local copies, waits for them, and re-layouts: 24.7 us -> 28.9 us
    all_gather x1, blocking collectives: 37.7 us -> 136 us  [shards(): totals = lax.all_gather(seg_total[None, :], 'seq', axis=0, tiled=True)]
    all_gather x1 -> x0, waiting for transfers between devices: 36.4 us -> none  [shards(): lax.all_gather(local_qg[None], 'seq', axis=0, tiled=True).astype(f32)]
    all_to_all x0 -> x1, starting transfers between devices: none -> 10.8 us  [shards(): lax.all_to_all(jnp.stack([local_qg[None]] * lax.axis_size('seq')), 'seq',...]
    all_to_all x1, starting transfers between devices: 8.2 us -> 12 us  [shards(): lax.all_to_all(grad_query, 'head', split_axis=0, concat_axis=1, tiled=True)]
    unnamed x27 -> x31, local copies, waits for them, and re-layouts: 9.06 us -> 9.04 us
  transfers between devices with their start and end apart: 11 -> 11, of which waited for: 9 -> 8; matrix products, arithmetic and copies ran while one was open for 27% -> 23% of each run, Pallas kernels for 0% -> 0%
where the time goes in v1:
time: 376 us; the launch traced here: 375 us
  blocking collectives  136 us (36%)
  waiting for transfers between devices  74.4 us (20%)
  starting transfers between devices  60.7 us (16%)
  matrix products  53.6 us (14%)
  local copies, waits for them, and re-layouts  28.9 us (8%)
  between operations  14.3 us (4%)
  other arithmetic  6.74 us (2%)
    all_gather x1, blocking collectives, shards(): totals = lax.all_gather(seg_total[None, :], 'seq', axis=0, tiled=True)  136 us
    all_to_all x1, waiting for transfers between devices, shards(): lax.all_to_all(query_in, 'head', split_axis=1, concat_axis=0, tiled=True)  13.7 us
    all_to_all x1, waiting for transfers between devices, shards(): lax.all_to_all(key_in, 'head', split_axis=1, concat_axis=0, tiled=True)  13.7 us
    all_to_all x1, starting transfers between devices, shards(): lax.all_to_all(grad_query, 'head', split_axis=0, concat_axis=1, tiled=True)  12 us
    all_to_all x1, waiting for transfers between devices, shards(): lax.all_to_all(grad_out, 'head', split_axis=1, concat_axis=0, tiled=True)  11.7 us
    all_to_all x1, waiting for transfers between devices, shards(): lax.all_to_all(value_in, 'head', split_axis=1, concat_axis=0, tiled=True)  10.9 us
    all_to_all x1, starting transfers between devices, shards(): lax.all_to_all(jnp.stack([local_qg[None]] * lax.axis_size('seq')), 'seq',...  10.8 us
    all_to_all x1, waiting for transfers between devices, shards(): lax.all_to_all(grad_value, 'head', split_axis=0, concat_axis=1, tiled=True)  9.9 us
  transfers between devices with their start and end apart: 11, of which 8 were waited for; matrix products, arithmetic and copies ran while one was open for 23% of the time, Pallas kernels for 0%

profile of v1, /device:TPU:1, one launch (start us, length us, event | category | flops | bytes accessed | tf_op | source)
XLA Modules:
  0.0 374.9 jit_solution(913253146165422030)
XLA Ops:
  7.2 6.6 %all-to-all-start.2 = ((bf16[128,8,4]{0,2,1:T(4,128)(2,1)}), bf16[128,8,4]{0,2,1:T(4,128)(2,1)S(1)}, u32[]{:S(2)}, u32[]{:S(2)}) async-start(bf16[128,8,4]{0,2,1:T(4,128)(2,1)} %bitcast.153), calls=%async_computation.2 | async-start | bytes 16384 | tf_op jit(solution)/shard_map/all_to_all | solution.py:17
  13.8 2.7 copy.118
  16.5 1.9 all-to-all-done.2
  18.4 4.2 %all-to-all-start = ((bf16[128,32,128]{2,0,1:T(8,128)(2,1)}), bf16[128,32,128]{2,0,1:T(8,128)(2,1)S(1)}, u32[]{:S(2)}, u32[]{:S(2)}) async-start(bf16[128,32,128]{2,0,1:T(8,128)(2,1)} %copy.118), calls=%async_computation | async-start | bytes 2097152 | tf_op jit(solution)/shard_map/all_to_all | solution.py:13
  22.6 1.4 copy.120
  24.0 13.7 %all-to-all-done = bf16[128,32,128]{2,0,1:T(8,128)(2,1)S(1)} async-done(((bf16[128,32,128]{2,0,1:T(8,128)(2,1)}), bf16[128,32,128]{2,0,1:T(8,128)(2,1)S(1)}, u32[]{:S(2)}, u32[]{:S(2)}) %all-to-all-start) | async-done | bytes 1048608 | tf_op jit(solution)/shard_map/all_to_all | solution.py:13
  37.7 4.3 %all-to-all-start.1 = ((bf16[128,32,128]{2,0,1:T(8,128)(2,1)}), bf16[128,32,128]{2,0,1:T(8,128)(2,1)S(1)}, u32[]{:S(2)}, u32[]{:S(2)}) async-start(bf16[128,32,128]{2,0,1:T(8,128)(2,1)} %copy.120), calls=%async_computation.1 | async-start | bytes 2097152 | tf_op jit(solution)/shard_map/all_to_all | solution.py:14
  42.0 1.4 copy.122
  43.4 13.7 %all-to-all-done.1 = bf16[128,32,128]{2,0,1:T(8,128)(2,1)S(1)} async-done(((bf16[128,32,128]{2,0,1:T(8,128)(2,1)}), bf16[128,32,128]{2,0,1:T(8,128)(2,1)S(1)}, u32[]{:S(2)}, u32[]{:S(2)}) %all-to-all-start.1) | async-done | bytes 1048608 | tf_op jit(solution)/shard_map/all_to_all | solution.py:14
  57.2 4.3 %all-to-all-start.3 = ((bf16[128,32,128]{2,0,1:T(8,128)(2,1)}), bf16[128,32,128]{2,0,1:T(8,128)(2,1)S(1)}, u32[]{:S(2)}, u32[]{:S(2)}) async-start(bf16[128,32,128]{2,0,1:T(8,128)(2,1)} %copy.122), calls=%async_computation.3 | async-start | bytes 2097152 | tf_op jit(solution)/shard_map/all_to_all | solution.py:15
  61.5 2.6 copy.132
  64.1 1.1 reduce-window.6
  65.7 10.9 %all-to-all-done.3 = bf16[128,32,128]{2,0,1:T(8,128)(2,1)S(1)} async-done(((bf16[128,32,128]{2,0,1:T(8,128)(2,1)}), bf16[128,32,128]{2,0,1:T(8,128)(2,1)S(1)}, u32[]{:S(2)}, u32[]{:S(2)}) %all-to-all-start.3) | async-done | bytes 1048608 | tf_op jit(solution)/shard_map/all_to_all | solution.py:15
  76.6 5.0 %all-to-all-start.5 = ((bf16[128,32,128]{2,0,1:T(8,128)(2,1)}), bf16[128,32,128]{2,0,1:T(8,128)(2,1)}, u32[]{:S(2)}, u32[]{:S(2)}) async-start(bf16[128,32,128]{2,0,1:T(8,128)(2,1)} %copy.132), calls=%async_computation.5 | async-start | bytes 2097152 | tf_op jit(solution)/shard_map/all_to_all | solution.py:16
  83.0 2.0 convolution_convert_fusion.1
  85.1 11.7 %all-to-all-done.5 = bf16[128,32,128]{2,0,1:T(8,128)(2,1)} async-done(((bf16[128,32,128]{2,0,1:T(8,128)(2,1)}), bf16[128,32,128]{2,0,1:T(8,128)(2,1)}, u32[]{:S(2)}, u32[]{:S(2)}) %all-to-all-start.5) | async-done | bytes 1048608 | tf_op jit(solution)/shard_map/all_to_all | solution.py:16
  96.8 1.3 copy.133
  98.1 1.3 convolution_convert_fusion
  99.4 3.0 stack.3
  102.5 10.8 %all-to-all-start.7 = ((bf16[32,1,4,128,128]{4,3,2,1,0:T(8,128)(2,1)}), bf16[32,1,4,128,128]{4,3,2,1,0:T(8,128)(2,1)}, u32[]{:S(2)}, u32[]{:S(2)}) async-start(bf16[32,1,4,128,128]{4,3,2,1,0:T(8,128)(2,1)} %stack.3), calls=%async_computation.7 | async-start | bytes 8388608 | tf_op jit(solution)/shard_map/all_to_all | solution.py:56
  113.3 1.3 iota_compare_fusion
  114.6 136.4 %all-gather.1 = f32[32,1,4]{2,1,0:T(1,128)S(1)} all-gather(f32[1,1,4]{2,1,0:T(1,128)S(1)} %bitcast.154), channel_id=1, replica_groups=mesh['seq'=32,'head'=8] {'seq'}, dimensions={0}, use_global_device_ids=true | all-gather | bytes 528 | tf_op jit(solution)/shard_map/all_gather | solution.py:36
  251.4 7.1 %multiply_convert_fusion = bf16[4,1024,1024]{2,1,0:T(8,128)(2,1)S(1)} fusion(bf16[1024,4,128]{2,0,1:T(8,128)(2,1)S(1)} %bitcast.119, bf16[1024,4,128]{2,0,1:T(8,128)(2,1)S(1)} %bitcast.140, f32[4,1024]{1,0:T(4,128)S(1)} %bitcast.149, pred[1024,1024]{1,0:T(8,128)(4,1)} %iota_compare_fusion), kind=kOutput, calls=%fused_computation | convolution fusion | flops 1098907648 | bytes 11550720 | tf_op jit(solution)/shard_map/the,she->hts/dot_general | solution.py:78
  258.5 4.0 %fusion.14 = f32[4,1024,128]{2,1,0:T(8,128)} fusion(bf16[4,1024,1024]{2,1,0:T(8,128)(2,1)S(1)} %multiply_convert_fusion, bf16[1024,4,128]{2,0,1:T(8,128)(2,1)S(1)} %bitcast.134), kind=kOutput, calls=%fused_computation.43 | convolution fusion | flops 1073741824 | bytes 11534336 | tf_op jit(solution)/shard_map/hts,shd->thd/dot_general | solution.py:81
  262.5 7.8 %multiply_convert_fusion.1 = bf16[4,1024,1024]{2,1,0:T(8,128)(2,1)} fusion(bf16[1024,4,128]{2,0,1:T(8,128)(2,1)S(1)} %bitcast.123, bf16[1024,4,128]{2,0,1:T(8,128)(2,1)S(1)} %bitcast.135, f32[4,1024]{1,0:T(4,128)S(1)} %bitcast.150, pred[1024,1024]{1,0:T(8,128)(4,1)S(1)} %copy-done.9), kind=kOutput, calls=%fused_computation.1 | convolution fusion | flops 1098907648 | bytes 11550720 | tf_op jit(solution)/shard_map/thd,shd->hts/dot_general | solution.py:71
  270.3 5.8 %fusion = f32[4,1,128,128]{3,1,2,0:T(1,128)S(1)} fusion(f32[32,4,1,1]{0,2,3,1:T(1,128)S(1)} %copy.148, bf16[32,4,128,128]{3,2,1,0:T(8,128)(2,1)} %bitcast.126), kind=kOutput, calls=%fused_computation.4 | convolution fusion | flops 25165824 | bytes 4456960 | tf_op jit(solution)/shard_map/ih,ihde->hde/dot_general | solution.py:46
  276.1 1.0 fusion.4
  277.1 1.8 copy.135
  278.9 12.0 %all-to-all-start.6 = ((bf16[1024,4,128]{2,1,0:T(4,128)(2,1)}), bf16[1024,4,128]{2,1,0:T(4,128)(2,1)S(1)}, u32[]{:S(2)}, u32[]{:S(2)}) async-start(bf16[1024,4,128]{2,1,0:T(4,128)(2,1)} %copy.135), calls=%async_computation.6 | async-start | bytes 2097152 | tf_op jit(solution)/shard_map/all_to_all | solution.py:94
  290.9 7.7 %fusion.15 = f32[4,1024,128]{2,1,0:T(8,128)} fusion(bf16[4,1024,1024]{2,1,0:T(8,128)(2,1)} %copy-done, bf16[1024,4,128]{2,0,1:T(8,128)(2,1)S(1)} %bitcast.124), kind=kOutput, calls=%fused_computation.44 | convolution fusion | flops 1073741824 | bytes 11534336 | tf_op jit(solution)/shard_map/hts,thd->shd/dot_general | solution.py:85
  298.6 3.7 multiply_reduce_fusion
  302.3 1.0 copy.162
  303.3 2.7 fusion.3
  306.0 1.8 copy.141
  307.8 4.8 %all-to-all-start.8 = ((bf16[1024,4,128]{2,1,0:T(4,128)(2,1)}), bf16[1024,4,128]{2,1,0:T(4,128)(2,1)}, u32[]{:S(2)}, u32[]{:S(2)}) async-start(bf16[1024,4,128]{2,1,0:T(4,128)(2,1)} %copy.141), calls=%async_computation.8 | async-start | bytes 2097152 | tf_op jit(solution)/shard_map/all_to_all | solution.py:95
  312.6 5.9 %fusion.13 = f32[4,1024,128]{2,1,0:T(8,128)S(1)} fusion(bf16[4,1024,1024]{2,1,0:T(8,128)(2,1)} %multiply_convert_fusion.1, bf16[1024,4,128]{2,0,1:T(8,128)(2,1)} %bitcast.139), kind=kOutput, calls=%fused_computation.42 | convolution fusion | flops 1073741824 | bytes 11534336 | tf_op jit(solution)/shard_map/hts,shd->thd/dot_general | solution.py:73
  319.6 1.8 copy.130
  321.4 6.5 %all-to-all-done.8 = bf16[1024,4,128]{2,1,0:T(4,128)(2,1)} async-done(((bf16[1024,4,128]{2,1,0:T(4,128)(2,1)}), bf16[1024,4,128]{2,1,0:T(4,128)(2,1)}, u32[]{:S(2)}, u32[]{:S(2)}) %all-to-all-start.8) | async-done | bytes 1048608 | tf_op jit(solution)/shard_map/all_to_all | solution.py:95
  327.8 4.3 %all-to-all-start.4 = ((bf16[1024,4,128]{2,1,0:T(4,128)(2,1)}), bf16[1024,4,128]{2,1,0:T(4,128)(2,1)S(1)}, u32[]{:S(2)}, u32[]{:S(2)}) async-start(bf16[1024,4,128]{2,1,0:T(4,128)(2,1)} %copy.130), calls=%async_computation.4 | async-start | bytes 2097152 | tf_op jit(solution)/shard_map/all_to_all | solution.py:93
  332.2 6.4 %fusion.16 = f32[4,1024,128]{2,1,0:T(8,128)S(1)} fusion(bf16[4,1024,1024]{2,1,0:T(8,128)(2,1)} %multiply_convert_fusion.1, bf16[1024,4,128]{2,0,1:T(8,128)(2,1)S(1)} %bitcast.121), kind=kOutput, calls=%fused_computation.45 | convolution fusion | flops 1073741824 | bytes 11534336 | tf_op jit(solution)/shard_map/hts,the->she/dot_general | solution.py:89
  339.6 1.8 copy.145
  341.4 5.9 %all-to-all-done.4 = bf16[1024,4,128]{2,1,0:T(4,128)(2,1)S(1)} async-done(((bf16[1024,4,128]{2,1,0:T(4,128)(2,1)}), bf16[1024,4,128]{2,1,0:T(4,128)(2,1)S(1)}, u32[]{:S(2)}, u32[]{:S(2)}) %all-to-all-start.4) | async-done | bytes 1048608 | tf_op jit(solution)/shard_map/all_to_all | solution.py:93
  347.3 4.3 %all-to-all-start.9 = ((bf16[1024,4,128]{2,1,0:T(4,128)(2,1)}), bf16[1024,4,128]{2,1,0:T(4,128)(2,1)S(1)}, u32[]{:S(2)}, u32[]{:S(2)}) async-start(bf16[1024,4,128]{2,1,0:T(4,128)(2,1)} %copy.145), calls=%async_computation.9 | async-start | bytes 2097152 | tf_op jit(solution)/shard_map/all_to_all | solution.py:96
  351.6 1.3 copy.136
  352.9 2.6 copy.142
  355.5 1.3 copy.131
  356.8 9.9 %all-to-all-done.9 = bf16[1024,4,128]{2,1,0:T(4,128)(2,1)S(1)} async-done(((bf16[1024,4,128]{2,1,0:T(4,128)(2,1)}), bf16[1024,4,128]{2,1,0:T(4,128)(2,1)S(1)}, u32[]{:S(2)}, u32[]{:S(2)}) %all-to-all-start.9) | async-done | bytes 1048608 | tf_op jit(solution)/shard_map/all_to_all | solution.py:96
  366.7 1.3 copy.146
  (51 shorter events, 4.4 us)
Async XLA Ops:
  7.2 15.4 %copy-start.7 = (bf16[128,32,128]{2,1,0:T(8,128)(2,1)S(1)}, bf16[128,32,128]{2,1,0:T(8,128)(2,1)}, u32[]{:S(2)}) copy-start(bf16[128,32,128]{2,1,0:T(8,128)(2,1)} %param.6) | copy-start | bytes 3145732
  7.2 11.3 %all-to-all-start.2 = ((bf16[128,8,4]{0,2,1:T(4,128)(2,1)}), bf16[128,8,4]{0,2,1:T(4,128)(2,1)S(1)}, u32[]{:S(2)}, u32[]{:S(2)}) async-start(bf16[128,8,4]{0,2,1:T(4,128)(2,1)} %bitcast.153), calls=%async_computation.2 | async-start | bytes 16384 | tf_op jit(solution)/shard_map/all_to_all | solution.py:17
  13.8 28.3 %copy-start.8 = (bf16[128,32,128]{2,1,0:T(8,128)(2,1)S(1)}, bf16[128,32,128]{2,1,0:T(8,128)(2,1)}, u32[]{:S(2)}) copy-start(bf16[128,32,128]{2,1,0:T(8,128)(2,1)} %param.7) | copy-start | bytes 3145732
  18.4 19.3 %all-to-all-start = ((bf16[128,32,128]{2,0,1:T(8,128)(2,1)}), bf16[128,32,128]{2,0,1:T(8,128)(2,1)S(1)}, u32[]{:S(2)}, u32[]{:S(2)}) async-start(bf16[128,32,128]{2,0,1:T(8,128)(2,1)} %copy.118), calls=%async_computation | async-start | bytes 2097152 | tf_op jit(solution)/shard_map/all_to_all | solution.py:13
  37.7 19.5 %all-to-all-start.1 = ((bf16[128,32,128]{2,0,1:T(8,128)(2,1)}), bf16[128,32,128]{2,0,1:T(8,128)(2,1)S(1)}, u32[]{:S(2)}, u32[]{:S(2)}) async-start(bf16[128,32,128]{2,0,1:T(8,128)(2,1)} %copy.120), calls=%async_computation.1 | async-start | bytes 2097152 | tf_op jit(solution)/shard_map/all_to_all | solution.py:14
  57.2 19.5 %all-to-all-start.3 = ((bf16[128,32,128]{2,0,1:T(8,128)(2,1)}), bf16[128,32,128]{2,0,1:T(8,128)(2,1)S(1)}, u32[]{:S(2)}, u32[]{:S(2)}) async-start(bf16[128,32,128]{2,0,1:T(8,128)(2,1)} %copy.122), calls=%async_computation.3 | async-start | bytes 2097152 | tf_op jit(solution)/shard_map/all_to_all | solution.py:15
  76.6 20.2 %all-to-all-start.5 = ((bf16[128,32,128]{2,0,1:T(8,128)(2,1)}), bf16[128,32,128]{2,0,1:T(8,128)(2,1)}, u32[]{:S(2)}, u32[]{:S(2)}) async-start(bf16[128,32,128]{2,0,1:T(8,128)(2,1)} %copy.132), calls=%async_computation.5 | async-start | bytes 2097152 | tf_op jit(solution)/shard_map/all_to_all | solution.py:16
  81.6 188.7 %all-gather.4.cloned.1.call-start = ((), (), s32[]{:S(2)}) async-start(), calls=%async_computation.10 | async-start | bytes 4325376 | tf_op jit(solution)/shard_map/all_gather | solution.py:49
  81.9 194.2 %copy-start.10 = (f32[1024,4]{0,1:T(4,128)}, f32[1024,4]{0,1:T(4,128)S(1)}, u32[]{:S(2)}) copy-start(f32[1024,4]{0,1:T(4,128)S(1)} %get-tuple-element.7) | copy-start | bytes 49156
  82.0 1.0 copy-start.1
  82.1 2.9 copy-start.4
  102.5 148.9 %copy-start.5 = (bf16[128,8,4,128]{3,0,1,2:T(8,128)(2,1)S(1)}, bf16[128,8,4,128]{3,0,1,2:T(8,128)(2,1)}, u32[]{:S(2)}) copy-start(bf16[128,8,4,128]{3,0,1,2:T(8,128)(2,1)} %copy-done.4) | copy-start | bytes 3145732
  102.5 176.4 %all-to-all-start.7 = ((bf16[32,1,4,128,128]{4,3,2,1,0:T(8,128)(2,1)}), bf16[32,1,4,128,128]{4,3,2,1,0:T(8,128)(2,1)}, u32[]{:S(2)}, u32[]{:S(2)}) async-start(bf16[32,1,4,128,128]{4,3,2,1,0:T(8,128)(2,1)} %stack.3), calls=%async_computation.7 | async-start | bytes 8388608 | tf_op jit(solution)/shard_map/all_to_all | solution.py:56
  251.4 7.1 %copy-start.2 = (bf16[128,8,4,128]{3,0,1,2:T(8,128)(2,1)S(1)}, bf16[128,8,4,128]{3,0,1,2:T(8,128)(2,1)}, u32[]{:S(2)}) copy-start(bf16[128,8,4,128]{3,0,1,2:T(8,128)(2,1)} %copy-done.1) | copy-start | bytes 3145732
  258.5 4.0 %copy-start = (bf16[4,1024,1024]{2,1,0:T(8,128)(2,1)}, bf16[4,1024,1024]{2,1,0:T(8,128)(2,1)S(1)}, u32[]{:S(2)}) copy-start(bf16[4,1024,1024]{2,1,0:T(8,128)(2,1)S(1)} %multiply_convert_fusion) | copy-start | bytes 25165828
  258.5 4.0 %copy-start.9 = (pred[1024,1024]{1,0:T(8,128)(4,1)S(1)}, pred[1024,1024]{1,0:T(8,128)(4,1)}, u32[]{:S(2)}) copy-start(pred[1024,1024]{1,0:T(8,128)(4,1)} %iota_compare_fusion) | copy-start | bytes 3145732
  270.3 5.9 %copy-start.6 = (f32[4,1024,128]{2,1,0:T(8,128)S(1)}, f32[4,1024,128]{2,1,0:T(8,128)}, u32[]{:S(2)}) copy-start(f32[4,1024,128]{2,1,0:T(8,128)} %fusion.14) | copy-start | bytes 6291460
  278.9 28.9 %all-to-all-start.6 = ((bf16[1024,4,128]{2,1,0:T(4,128)(2,1)}), bf16[1024,4,128]{2,1,0:T(4,128)(2,1)S(1)}, u32[]{:S(2)}, u32[]{:S(2)}) async-start(bf16[1024,4,128]{2,1,0:T(4,128)(2,1)} %copy.135), calls=%async_computation.6 | async-start | bytes 2097152 | tf_op jit(solution)/shard_map/all_to_all | solution.py:94
  307.8 20.0 %all-to-all-start.8 = ((bf16[1024,4,128]{2,1,0:T(4,128)(2,1)}), bf16[1024,4,128]{2,1,0:T(4,128)(2,1)}, u32[]{:S(2)}, u32[]{:S(2)}) async-start(bf16[1024,4,128]{2,1,0:T(4,128)(2,1)} %copy.141), calls=%async_computation.8 | async-start | bytes 2097152 | tf_op jit(solution)/shard_map/all_to_all | solution.py:95
  312.6 6.0 %copy-start.11 = (f32[1024,4]{0,1:T(4,128)S(1)}, f32[1024,4]{0,1:T(4,128)}, u32[]{:S(2)}) copy-start(f32[1024,4]{0,1:T(4,128)} %copy-done.10) | copy-start | bytes 49156
  327.8 19.5 %all-to-all-start.4 = ((bf16[1024,4,128]{2,1,0:T(4,128)(2,1)}), bf16[1024,4,128]{2,1,0:T(4,128)(2,1)S(1)}, u32[]{:S(2)}, u32[]{:S(2)}) async-start(bf16[1024,4,128]{2,1,0:T(4,128)(2,1)} %copy.130), calls=%async_computation.4 | async-start | bytes 2097152 | tf_op jit(solution)/shard_map/all_to_all | solution.py:93
  332.2 6.4 %copy-start.3 = (bf16[128,8,4,128]{3,0,1,2:T(8,128)(2,1)S(1)}, bf16[128,8,4,128]{3,0,1,2:T(8,128)(2,1)}, u32[]{:S(2)}) copy-start(bf16[128,8,4,128]{3,0,1,2:T(8,128)(2,1)} %copy-done.1) | copy-start | bytes 3145732
  347.3 19.5 %all-to-all-start.9 = ((bf16[1024,4,128]{2,1,0:T(4,128)(2,1)}), bf16[1024,4,128]{2,1,0:T(4,128)(2,1)S(1)}, u32[]{:S(2)}, u32[]{:S(2)}) async-start(bf16[1024,4,128]{2,1,0:T(4,128)(2,1)} %copy.145), calls=%async_computation.9 | async-start | bytes 2097152 | tf_op jit(solution)/shard_map/all_to_all | solution.py:96
Sparse Core Ops, SparseCore 0:
  85.6 136.5 all-gather.3
